TPU v7x, 128 devices: a whole 4x4x4 slice. The times are simulated.
128 devices in a mesh: seq: 32 (over x, y, core), head: 4 (over z).
Axes of the slice: x: 4, y: 4, z: 4, core: 2. Of those that a mesh axis runs over, the one named last changes fastest.
Arguments:
- vis_tokens: bfloat16 [12288, 1408], P('seq'), may hold values from -70 to 70
- vis_counts: int32 [4, 8], replicated, may hold values from 1 to 384, 1536 in all within a row
- vis_spatial: int32 [4, 96], replicated, may hold values from 0 to 1023, as said below
- enc_gain: float32 [1408], replicated, may hold values from 0.25 to 1.75
- enc_bias: float32 [1408], replicated, may hold values from -3 to 3
- enc_qkv: bfloat16 [3, 1408, 1408], P(None, None, 'head'), may hold values from -6 to 6
- enc_proj: bfloat16 [1408, 1408], P('head'), may hold values from -0.15625 to 0.15625
- final_gain: float32 [1408], replicated, may hold values from 0.25 to 1.75
- final_bias: float32 [1408], replicated, may hold values from -3 to 3
- to_decoder: bfloat16 [1408, 512], replicated, may hold values from -0.15625 to 0.15625
- mask_token: float32 [512], replicated, may hold values from -4 to 4
- dec_gain: float32 [512], replicated, may hold values from 0.25 to 1.75
- dec_bias: float32 [512], replicated, may hold values from -3 to 3
- dec_qkv: bfloat16 [3, 512, 512], P(None, None, 'head'), may hold values from -11 to 11
Outputs:
- decoded: bfloat16 [4, 16, 1024, 512], P(None, None, 'seq', 'head')
Inputs may be any that keep to these rules, and one draw needn't show every extreme that they name: `vis_spatial`: row c lists in increasing order the spatial positions visible in every frame of clip c; each aligned run of 32 spatial positions holds exactly 3 of them. The visible tokens of clip c, in order of position, lie on the members of its encoder group in order, vis_counts[c, g] of them on member g; each row sums to 1536.
All inputs are finite; a program needn't handle non-finite values.
Results may differ from a plain program's by a relative error of at most 0.015.
Values may be sent and summed in bfloat16 or wider, within the bound.
A program may use at most 320 MiB of HBM per device.

v0:
```python
import math
import jax
import jax.numpy as jnp
from jax import lax
from jax.sharding import PartitionSpec as P

D = 1408
HEADS = 16
DD = 512
DHEADS = 8
S = 1024
BLOCK = 32
GROUP = 8
L = 16384
VSP = 96
VIS = 1536
epsilon = 1e-06
floor_score = -1e30


def from_partner(block, axis, distance):
    count = lax.axis_size(axis)
    route = []
    for low in range(count):
        high = low | 1 << distance
        if high != low and high < count:
            route += [(low, high), (high, low)]
    return lax.ppermute(block, axis, route)


def layer_norm(values, gain_row, bias_row):
    centre = jnp.mean(values, axis=-1, keepdims=True)
    centred = values - centre
    spread = jnp.mean(centred * centred, axis=-1, keepdims=True)
    return centred * lax.rsqrt(spread + epsilon) * gain_row + bias_row


def sinusoid(positions, table_width):
    column_ids = jnp.arange(table_width, dtype=jnp.int32)
    exponent = (2 * (column_ids // 2)).astype(jnp.float32) / table_width
    frequency = jnp.exp(exponent * -math.log(10000.0))
    angles = positions.astype(jnp.float32)[:, None] * frequency[None, :]
    return jnp.where(column_ids[None, :] % 2 == 0, jnp.sin(angles), jnp.cos(angles))


def fold_block(fold_state, queries, key_rows, value_rows, allowed, score_scale):
    running_max, running_sum, running_acc = fold_state
    scores = jnp.einsum("cqhe,ckhe->chqk", queries, key_rows, preferred_element_type=jnp.float32)
    allowed_grid = allowed[:, None, None, :]
    scores = jnp.where(allowed_grid, scores * score_scale, floor_score)
    new_max = jnp.maximum(running_max, jnp.max(scores, axis=-1))
    factor = jnp.exp(running_max - new_max)
    raised = jnp.where(allowed_grid, jnp.exp(scores - new_max[..., None]), 0.0)
    running_sum = running_sum * factor + jnp.sum(raised, axis=-1)
    weights = raised.astype(jnp.bfloat16)
    update = jnp.einsum("chqk,ckhe->chqe", weights, value_rows, preferred_element_type=jnp.float32)
    running_acc = running_acc * factor[..., None] + update
    return (new_max, running_sum, running_acc)


def empty_state(batch_count, head_count, query_count, head_size):
    return (
        jnp.full((batch_count, head_count, query_count), floor_score, jnp.float32),
        jnp.zeros((batch_count, head_count, query_count), jnp.float32),
        jnp.zeros((batch_count, head_count, query_count, head_size), jnp.float32),
    )


def body(
    vis_tokens,
    vis_counts,
    vis_spatial,
    enc_gain,
    enc_bias,
    enc_qkv,
    enc_proj,
    final_gain,
    final_bias,
    to_decoder,
    mask_token,
    dec_gain,
    dec_bias,
    dec_qkv,
):
    seq_count = lax.axis_size("seq")
    seq_index = lax.axis_index("seq")
    clips = vis_counts.shape[0]
    clip_index = seq_index % clips
    member = seq_index // clips
    slot_count = vis_tokens.shape[0]
    slot_ids = jnp.arange(slot_count, dtype=jnp.int32)
    member_ids = jnp.arange(GROUP, dtype=jnp.int32)
    group_counts = lax.dynamic_index_in_dim(vis_counts, clip_index, 0, keepdims=False)
    before = jnp.sum(jnp.where(member_ids < member, group_counts, 0))
    slot_live = slot_ids < jnp.sum(jnp.where(member_ids == member, group_counts, 0))
    token_rows = vis_tokens.astype(jnp.float32)
    normed = layer_norm(token_rows, enc_gain, enc_bias).astype(jnp.bfloat16)
    enc_parts = [
        jnp.dot(normed, enc_qkv[part_id], preferred_element_type=jnp.float32).astype(jnp.bfloat16)
        for part_id in range(3)
    ]
    head_size = D // HEADS
    enc_width = enc_parts[0].shape[1]
    local_heads = enc_width // head_size
    enc_queries = enc_parts[0].reshape(1, slot_count, local_heads, head_size)
    key_value = jnp.stack([enc_parts[1], enc_parts[2]])
    enc_scale = 1.0 / math.sqrt(head_size)
    clip_bits = clips.bit_length() - 1
    collected = key_value[None]
    for bit in range(GROUP.bit_length() - 1):
        partner = from_partner(collected, "seq", bit + clip_bits)
        upper_side = (member >> bit) % 2 == 1
        collected = jnp.where(
            upper_side,
            jnp.concatenate([partner, collected], axis=0),
            jnp.concatenate([collected, partner], axis=0),
        )
    group_keys = jnp.moveaxis(collected, 1, 0).reshape(
        2, 1, GROUP * slot_count, local_heads, head_size
    )
    group_live = (slot_ids[None, :] < group_counts[:, None]).reshape(1, GROUP * slot_count)
    fold_state = fold_block(
        empty_state(1, local_heads, slot_count, head_size),
        enc_queries,
        group_keys[0],
        group_keys[1],
        group_live,
        enc_scale,
    )
    context = fold_state[2][0] / fold_state[1][0][..., None]
    context = jnp.transpose(context, (1, 0, 2)).reshape(slot_count, enc_width).astype(jnp.bfloat16)
    partial_out = jnp.dot(context, enc_proj, preferred_element_type=jnp.float32)
    attended = lax.psum(partial_out.astype(jnp.bfloat16), "head").astype(jnp.float32)
    residual = token_rows + attended
    final_rows = layer_norm(residual, final_gain, final_bias).astype(jnp.bfloat16)
    encoded = jnp.dot(final_rows, to_decoder, preferred_element_type=jnp.float32).astype(
        jnp.bfloat16
    )
    visible_index = jnp.minimum(before + slot_ids, VIS - 1)
    spatial_row = lax.dynamic_index_in_dim(vis_spatial, clip_index, 0, keepdims=False)
    spatial_ids = jnp.arange(VSP, dtype=jnp.int32)
    spatial = jnp.sum(
        jnp.where((visible_index % VSP)[:, None] == spatial_ids[None, :], spatial_row[None, :], 0),
        axis=1,
    )
    position = visible_index // VSP * S + spatial
    block_index = position // BLOCK
    owner_index = block_index % seq_count
    own_rows = L // seq_count
    local_row = clip_index * own_rows + block_index // seq_count * BLOCK + position % BLOCK
    per_peer = slot_count // seq_count
    peer_ids = jnp.arange(seq_count, dtype=jnp.int32)
    owner_hits = ((owner_index[:, None] == peer_ids[None, :]) & slot_live[:, None]).astype(
        jnp.float32
    )
    earlier_mask = (slot_ids[None, :] < slot_ids[:, None]).astype(jnp.float32)
    earlier = jnp.dot(earlier_mask, owner_hits, precision=lax.Precision.HIGHEST)
    bucket_rank = jnp.sum(earlier * owner_hits, axis=1).astype(jnp.int32)
    target = jnp.where(slot_live, owner_index * per_peer + bucket_rank, -1)
    bucket_ids = jnp.arange(seq_count * per_peer, dtype=jnp.int32)
    chosen = target[None, :] == bucket_ids[:, None]
    send_rows = (
        jnp.dot(chosen.astype(jnp.bfloat16), encoded, preferred_element_type=jnp.float32)
        .astype(jnp.bfloat16)
        .reshape(seq_count, per_peer, DD)
    )
    send_index = jnp.max(jnp.where(chosen, local_row[None, :], -1), axis=1).reshape(
        seq_count, per_peer
    )
    got_rows, got_index = (
        lax.all_to_all(send_rows, "seq", split_axis=0, concat_axis=0, tiled=True),
        lax.all_to_all(send_index, "seq", split_axis=0, concat_axis=0, tiled=True),
    )
    total_rows = clips * own_rows
    got_index = jnp.where(got_index < 0, total_rows, got_index).reshape(-1)
    placed = (
        jnp.zeros((total_rows, DD), jnp.float32)
        .at[got_index]
        .set(got_rows.reshape(-1, DD).astype(jnp.float32), mode="drop")
    )
    row_ids = jnp.arange(own_rows, dtype=jnp.int32)
    local_position = (row_ids // BLOCK * seq_count + seq_index) * BLOCK + row_ids % BLOCK
    frame_ids = jnp.arange(S, dtype=jnp.int32)
    spatial_flags = jnp.any(vis_spatial[:, :, None] == frame_ids[None, None, :], axis=1)
    column_pick = ((local_position % S)[:, None] == frame_ids[None, :]).astype(jnp.float32)
    seen_flags = (
        jnp.einsum(
            "cs,rs->cr",
            spatial_flags.astype(jnp.float32),
            column_pick,
            precision=lax.Precision.HIGHEST,
        )
        > 0.5
    )
    inputs = sinusoid(local_position, DD)[None] + jnp.where(
        seen_flags[..., None], placed.reshape(clips, own_rows, DD), mask_token[None, None, :]
    )
    dec_normed = layer_norm(inputs, dec_gain, dec_bias).astype(jnp.bfloat16)
    dec_size = DD // DHEADS
    dec_query = jnp.einsum(
        "crd,de->cre", dec_normed, dec_qkv[0], preferred_element_type=jnp.float32
    ).astype(jnp.bfloat16)
    dec_width = dec_query.shape[2]
    dec_heads = dec_width // dec_size
    dec_queries = dec_query.reshape(clips, own_rows, dec_heads, dec_size)
    dec_scale = 1.0 / math.sqrt(dec_size)
    start_state = empty_state(clips, dec_heads, own_rows, dec_size)
    dec_key = jnp.einsum(
        "crd,de->cre", dec_normed, dec_qkv[1], preferred_element_type=jnp.float32
    ).astype(jnp.bfloat16)
    dec_value = jnp.einsum(
        "crd,de->cre", dec_normed, dec_qkv[2], preferred_element_type=jnp.float32
    ).astype(jnp.bfloat16)
    stacked = jnp.stack([dec_key, dec_value])
    shard_part = lax.all_gather(stacked, "seq", axis=2, tiled=True)
    row_count = shard_part.shape[2]
    block_count = row_count // own_rows
    block_rows = row_count // block_count
    grouped = jnp.moveaxis(
        shard_part.reshape(2, clips, block_count, block_rows, dec_heads, dec_size), 2, 0
    )
    everywhere = jnp.ones((clips, block_rows), dtype=bool)

    def scan_step(inner_state, key_block):
        return (
            fold_block(inner_state, dec_queries, key_block[0], key_block[1], everywhere, dec_scale),
            None,
        )

    result_state, _ = lax.scan(scan_step, start_state, grouped)
    fold_state = result_state
    dec_context = fold_state[2] / fold_state[1][..., None]
    dec_context = jnp.transpose(dec_context, (0, 2, 1, 3)).reshape(
        clips, own_rows // BLOCK, BLOCK, dec_width
    )
    return dec_context.astype(jnp.bfloat16)


def solution(mesh):
    in_specs = (
        P("seq", None),
        P(),
        P(),
        P(),
        P(),
        P(None, None, "head"),
        P("head", None),
        P(),
        P(),
        P(),
        P(),
        P(),
        P(),
        P(None, None, "head"),
    )
    out_specs = P(None, None, "seq", "head")
    return jax.shard_map(body, mesh=mesh, in_specs=in_specs, out_specs=out_specs, check_vma=False)
```

profile of v0, /device:TPU:1, one launch (start us, length us, event | category | flops | bytes accessed | tf_op | source)
XLA Modules:
  0.0 682.2 jit_solution(31880487049167066)
XLA Ops:
  14.1 3.8 collective-permute-start
  17.9 11.9 %collective-permute-done = bf16[1,2,384,352]{2,3,1,0:T(8,128)(2,1)} collective-permute-done((bf16[1,2,384,352]{2,3,1,0:T(8,128)(2,1)S(1)}, bf16[1,2,384,352]{2,3,1,0:T(8,128)(2,1)}, u32[]{:S(2)}, u32[]{:S(2)}) %collective-permute-start) | collective-permute-done | bytes 540704 | tf_op jit(solution)/shard_map/ppermute | solution.py:28
  33.3 23.1 %collective-permute-done.1 = bf16[2,2,384,352]{2,3,1,0:T(8,128)(2,1)} collective-permute-done((bf16[2,2,384,352]{2,3,1,0:T(8,128)(2,1)}, bf16[2,2,384,352]{2,3,1,0:T(8,128)(2,1)}, u32[]{:S(2)}, u32[]{:S(2)}) %collective-permute-start.1) | collective-permute-done | bytes 1081376 | tf_op jit(solution)/shard_map/ppermute | solution.py:28
  56.4 4.0 maximum_select_fusion.1
  68.0 40.4 %collective-permute-done.2 = bf16[4,2,384,352]{2,3,1,0:T(8,128)(2,1)} collective-permute-done((bf16[4,2,384,352]{2,3,1,0:T(8,128)(2,1)}, bf16[4,2,384,352]{2,3,1,0:T(8,128)(2,1)}, u32[]{:S(2)}, u32[]{:S(2)}) %collective-permute-start.2) | collective-permute-done | bytes 2162720 | tf_op jit(solution)/shard_map/ppermute | solution.py:28
  108.5 3.9 fusion.22
  116.3 4.2 reshape.477
  120.5 3.7 copy.37
  124.2 4.7 reshape.478
  128.9 11.2 %fusion.16 = (f32[4,384]{1,0:T(4,128)S(1)}, f32[4,384,3072]{2,1,0:T(8,128)}) fusion(pred[3072]{0:T(1024)(128)(4,1)S(1)} %lt.153, bf16[384,4,88]{0,2,1:T(8,128)(2,1)S(1)} %bitcast.138, bf16[3072,4,88]{0,2,1:T(8,128)(2,1)} %reshape.477), kind=kOutput, calls=%fused_computation.24 | convolution fusion | flops 844626432 | bytes 21316608 | tf_op jit(solution)/shard_map/cqhe,ckhe->chqk/dot_general | solution.py:48
  140.1 11.2 %fusion.17 = f32[4,384]{1,0:T(4,128)S(1)} fusion(f32[4,384,3072]{2,1,0:T(8,128)} %get-tuple-element.105, f32[4,384]{1,0:T(4,128)S(1)} %get-tuple-element.103, pred[3072]{0:T(1024)(128)(4,1)S(1)} %lt.153), kind=kLoop, calls=%fused_computation.25 | loop fusion | flops 23591424 | bytes 18889728 | tf_op jit(solution)/shard_map/reduce_sum | solution.py:54
  151.4 12.2 %fusion.62 = bf16[384,4,88]{0,2,1:T(8,128)(2,1)} fusion(bf16[3072,4,88]{0,2,1:T(8,128)(2,1)} %reshape.478, f32[4,384,3072]{2,1,0:T(8,128)} %get-tuple-element.105, f32[4,384]{1,0:T(4,128)S(1)} %get-tuple-element.103, pred[3072]{0:T(1024)(128)(4,1)S(1)} %lt.153, f32[384,4]{0,1:T(4,128)S(1)} %bitcast_add_fusion.1, f32[384,4]{0,1:T(4,128)S(1)} %get-tuple-element.102), kind=kOutput, calls=%fused_computation.86 | convolution fusion | flops 854470656 | bytes 21328896 | tf_op jit(solution)/shard_map/chqk,ckhe->chqe/dot_general | solution.py:56
  168.7 10.2 %all-to-all-start = ((s32[32,1,12]{2,1,0:T(1,128)}), s32[32,1,12]{2,1,0:T(1,128)S(1)}, u32[]{:S(2)}, u32[]{:S(2)}) async-start(s32[32,1,12]{2,1,0:T(1,128)} %bitcast.3), calls=%async_computation | async-start | bytes 32768 | tf_op jit(solution)/shard_map/all_to_all | solution.py:172
  179.9 36.2 %all-reduce.2.cloned.1.call-done = bf16[384,1408]{1,0:T(8,128)(2,1)} async-done(((bf16[384,1408]{1,0:T(8,128)(2,1)}), bf16[384,1408]{1,0:T(8,128)(2,1)}) %all-reduce.2.cloned.1.call-update) | async-done | bytes 1081360 | tf_op jit(solution)/shard_map/psum | solution.py:133
  221.6 9.3 %all-to-all-start.1 = ((bf16[32,12,512]{2,1,0:T(8,128)(2,1)}), bf16[32,12,512]{2,1,0:T(8,128)(2,1)S(1)}, u32[]{:S(2)}, u32[]{:S(2)}) async-start(bf16[32,12,512]{2,1,0:T(8,128)(2,1)} %reshape.479), calls=%async_computation.1 | async-start | bytes 1048576 | tf_op jit(solution)/shard_map/all_to_all | solution.py:171
  231.0 3.7 fusion.57
  236.2 6.3 all-to-all-done.1
  242.6 4.0 scatter_custom_fusion
  246.6 3.0 fusion.23
  257.6 108.6 %all-gather.2.cloned.1.call-done = bf16[2,4,16384,128]{3,2,1,0:T(8,128)(2,1)} async-done(((bf16[2,4,512,128]{3,2,1,0:T(8,128)(2,1)}), bf16[2,4,16384,128]{3,2,1,0:T(8,128)(2,1)}) %all-gather.2.cloned.1.call-update) | async-done | bytes 33554448 | tf_op jit(solution)/shard_map/all_gather | solution.py:215
  366.1 44.1 %copy.38 = bf16[2,4,16384,128]{2,3,1,0:T(8,128)(2,1)} copy(bf16[2,4,16384,128]{3,2,1,0:T(8,128)(2,1)} %all-gather.2.cloned.1.call-done) | data formatting | bytes 67108864 | tf_op jit(solution)/shard_map/all_gather | solution.py:215
  410.2 22.7 %copy.45 = bf16[128,8,32,512]{3,2,1,0:T(8,128)(2,1)} copy(bf16[128,8,32,512]{3,1,2,0:T(8,128)(2,1)} %bitcast.132) | data formatting | bytes 67108864
  432.9 22.9 %copy.40 = bf16[32,2,4,512,2,64]{3,5,4,2,1,0:T(8,128)(2,1)} copy(bf16[32,2,4,512,2,64]{3,0,5,4,2,1:T(8,128)(2,1)} %bitcast.133) | data formatting | bytes 67108864
  455.8 217.1 %while.15 = (s32[]{:T(128)}, f32[4,2,512]{2,1,0:T(2,128)S(1)}, f32[4,2,512]{2,1,0:T(2,128)S(1)}, f32[4,2,512,64]{2,3,1,0:T(8,128)S(1)}, bf16[32,2,4,512,2,64]{3,...) while((s32[]{:T(128)}, f32[4,2,512]{2,1,0:T(2,128)S(1)}, ...), condition=%wide.region_19.20_spmd.clone, body=%wide.region_16.19_spmd.clone.sunk | while | flops 554455040 | bytes 29098120 | solution.py:230
  480.0 2.9 fusion.145
  500.4 2.9 fusion.145
  527.5 2.9 fusion.145
  547.9 2.9 fusion.145
  575.0 2.9 fusion.145
  595.4 2.9 fusion.145
  622.5 2.9 fusion.145
  670.0 2.9 fusion.145
  (282 shorter events, 238.1 us)
Async XLA Ops:
  6.5 211.8 %copy-start = (bf16[1408,512]{1,0:T(8,128)(2,1)S(1)}, bf16[1408,512]{1,0:T(8,128)(2,1)}, u32[]{:S(2)}) copy-start(bf16[1408,512]{1,0:T(8,128)(2,1)} %param.25) | copy-start | bytes 4325380
  6.5 3.3 copy-start.4
  6.5 3.3 copy-start.12
  6.5 3.3 copy-start.13
  6.5 209.5 %all-reduce.2.cloned.1.call-start = ((), (), s32[]{:S(2)}) async-start(), calls=%async_computation.2 | async-start | bytes 2162688 | tf_op jit(solution)/shard_map/psum | solution.py:133
  14.1 15.7 %collective-permute-start = (bf16[1,2,384,352]{2,3,1,0:T(8,128)(2,1)S(1)}, bf16[1,2,384,352]{2,3,1,0:T(8,128)(2,1)}, u32[]{:S(2)}, u32[]{:S(2)}) collective-permute-start(bf16[1,2,384,352]{2,3,1,0:T(8,128)(2,1)S(1)} %maximum_bitcast_fusion), channel_id=1, source_target_pairs={{0,16},{16,0},{4,20},{20,4},{8,24},{24,8},{12,28},{28,12},{32,48},... | collective-permute-start | bytes 1622024 | tf_op jit(solution)/shard_map/ppermute | solution.py:28
  32.2 24.3 %collective-permute-start.1 = (bf16[2,2,384,352]{2,3,1,0:T(8,128)(2,1)}, bf16[2,2,384,352]{2,3,1,0:T(8,128)(2,1)}, u32[]{:S(2)}, u32[]{:S(2)}) collective-permute-start(bf16[2,2,384,352]{2,3,1,0:T(8,128)(2,1)} %maximum_select_fusion.2), channel_id=1, source_target_pairs={{0,32},{32,0},{4,36},{36,4},{8,40},{40,8},{12,44},{44,12},{16,48},... | collective-permute-start | bytes 3244040 | tf_op jit(solution)/shard_map/ppermute | solution.py:28
  33.3 31.1 %copy-start.11 = (s32[4,96]{1,0:T(4,128)S(1)}, s32[4,96]{1,0:T(4,128)}, u32[]{:S(2)}) copy-start(s32[4,96]{1,0:T(4,128)} %param.18) | copy-start | bytes 4612
  60.4 48.1 %collective-permute-start.2 = (bf16[4,2,384,352]{2,3,1,0:T(8,128)(2,1)}, bf16[4,2,384,352]{2,3,1,0:T(8,128)(2,1)}, u32[]{:S(2)}, u32[]{:S(2)}) collective-permute-start(bf16[4,2,384,352]{2,3,1,0:T(8,128)(2,1)} %maximum_select_fusion.1), channel_id=1, source_target_pairs={{0,64},{64,0},{4,68},{68,4},{8,72},{72,8},{12,76},{76,12},{16,80},... | collective-permute-start | bytes 6488072 | tf_op jit(solution)/shard_map/ppermute | solution.py:28
  151.4 12.2 %copy-start.6 = (bf16[352,1408]{1,0:T(8,128)(2,1)S(1)}, bf16[352,1408]{1,0:T(8,128)(2,1)}, u32[]{:S(2)}) copy-start(bf16[352,1408]{1,0:T(8,128)(2,1)} %param.22) | copy-start | bytes 2973700
  168.7 52.9 %all-to-all-start = ((s32[32,1,12]{2,1,0:T(1,128)}), s32[32,1,12]{2,1,0:T(1,128)S(1)}, u32[]{:S(2)}, u32[]{:S(2)}) async-start(s32[32,1,12]{2,1,0:T(1,128)} %bitcast.3), calls=%async_computation | async-start | bytes 32768 | tf_op jit(solution)/shard_map/all_to_all | solution.py:172
  179.8 38.5 %copy-start.14 = (f32[1408]{0:T(1024)S(1)}, f32[1408]{0:T(1024)}, u32[]{:S(2)}) copy-start(f32[1408]{0:T(1024)} %param.24) | copy-start | bytes 16900
  179.8 38.5 %copy-start.15 = (f32[1408]{0:T(1024)S(1)}, f32[1408]{0:T(1024)}, u32[]{:S(2)}) copy-start(f32[1408]{0:T(1024)} %param.23) | copy-start | bytes 16900
  216.1 1.7 copy-start.5
  221.6 20.9 %all-to-all-start.1 = ((bf16[32,12,512]{2,1,0:T(8,128)(2,1)}), bf16[32,12,512]{2,1,0:T(8,128)(2,1)S(1)}, u32[]{:S(2)}, u32[]{:S(2)}) async-start(bf16[32,12,512]{2,1,0:T(8,128)(2,1)} %reshape.479), calls=%async_computation.1 | async-start | bytes 1048576 | tf_op jit(solution)/shard_map/all_to_all | solution.py:171
  230.9 135.2 %all-gather.2.cloned.1.call-start = ((), (), s32[]{:S(2)}) async-start(), calls=%async_computation.3 | async-start | bytes 34603008 | tf_op jit(solution)/shard_map/all_gather | solution.py:215
  242.6 4.0 copy-start.8
  246.6 3.4 copy-start.2
  250.0 1.3 copy-start.9
  250.0 1.3 copy-start.10
  251.4 1.2 copy-start.7
  252.6 1.4 copy-start.3
  672.9 2.2 copy-start.1
Sparse Core Ops, SparseCore 0:
  166.5 49.5 all-reduce.1
  255.2 110.8 all-gather.1
where the time goes:
time: 693 us; the launch traced here: 682 us
  waiting for transfers between devices  227 us (33%)
  matrix products  207 us (30%)
  local copies, waits for them, and re-layouts  115 us (17%)
  other arithmetic  90.4 us (13%)
  starting transfers between devices  27.2 us (4%)
  between operations  14.1 us (2%)
    all_gather x1, waiting for transfers between devices, body(): shard_part = lax.all_gather(stacked, 'seq', axis=2, tiled=True)  109 us
    dot_general x33, matrix products, fold_block(): jnp.einsum('chqk,ckhe->chqe', weights, value_rows, preferred_element_type...  105 us
    dot_general x33, matrix products, fold_block(): jnp.einsum('cqhe,ckhe->chqk', queries, key_rows, preferred_element_type=j...  86.7 us
    ppermute x3, waiting for transfers between devices, from_partner(): return lax.ppermute(block, axis, route)  75.4 us
    reduce_sum x33, other arithmetic, fold_block(): running_sum = running_sum * factor + jnp.sum(raised, axis=-1)  56.9 us
    unnamed x35, local copies, waits for them, and re-layouts  46.1 us
    all_gather x1, local copies, waits for them, and re-layouts, body(): shard_part = lax.all_gather(stacked, 'seq', axis=2, tiled=True)  44.1 us
    psum x1, waiting for transfers between devices, body(): lax.psum(partial_out.astype(jnp.bfloat16), 'head').astype(jnp.float32)  36.2 us
  transfers between devices with their start and end apart: 7, of which 6 were waited for; matrix products, arithmetic and copies ran while one was open for 3% of the time, Pallas kernels for 0%

commit v1 on v0

--- a/solution.py
+++ b/solution.py
@@ -212,7 +212,7 @@
         "crd,de->cre", dec_normed, dec_qkv[2], preferred_element_type=jnp.float32
     ).astype(jnp.bfloat16)
     stacked = jnp.stack([dec_key, dec_value])
-    shard_part = lax.all_gather(stacked, "seq", axis=2, tiled=True)
+    shard_part = jnp.concatenate(lax.all_gather(stacked, "seq"), axis=2)
     row_count = shard_part.shape[2]
     block_count = row_count // own_rows
     block_rows = row_count // block_count

time: 693 us -> 648 us (0.935)
  local copies, waits for them, and re-layouts: 115 us -> 69.7 us
    unnamed x35 -> x33, local copies, waits for them, and re-layouts: 46.1 us -> 0.49 us
    reshape x0 -> x1, local copies, waits for them, and re-layouts: none -> 44.2 us  [body(): shard_part = jnp.concatenate(lax.all_gather(stacked, 'seq'), axis=2)]
    all_gather x1 -> x0, local copies, waits for them, and re-layouts: 44.1 us -> none  [body(): shard_part = lax.all_gather(stacked, 'seq', axis=2, tiled=True)]
where the time goes in v1:
time: 648 us; the launch traced here: 637 us
  waiting for transfers between devices  227 us (35%)
  matrix products  207 us (32%)
  other arithmetic  90.4 us (14%)
  local copies, waits for them, and re-layouts  69.7 us (11%)
  starting transfers between devices  27.2 us (4%)
  between operations  14.1 us (2%)
    all_gather x1, waiting for transfers between devices, body(): shard_part = jnp.concatenate(lax.all_gather(stacked, 'seq'), axis=2)  109 us
    dot_general x33, matrix products, fold_block(): jnp.einsum('chqk,ckhe->chqe', weights, value_rows, preferred_element_type...  105 us
    dot_general x33, matrix products, fold_block(): jnp.einsum('cqhe,ckhe->chqk', queries, key_rows, preferred_element_type=j...  86.7 us
    ppermute x3, waiting for transfers between devices, from_partner(): return lax.ppermute(block, axis, route)  75.4 us
    reduce_sum x33, other arithmetic, fold_block(): running_sum = running_sum * factor + jnp.sum(raised, axis=-1)  56.9 us
    reshape x1, local copies, waits for them, and re-layouts, body(): shard_part = jnp.concatenate(lax.all_gather(stacked, 'seq'), axis=2)  44.2 us
    psum x1, waiting for transfers between devices, body(): lax.psum(partial_out.astype(jnp.bfloat16), 'head').astype(jnp.float32)  36.2 us
  transfers between devices with their start and end apart: 7, of which 6 were waited for; matrix products, arithmetic and copies ran while one was open for 3% of the time, Pallas kernels for 0%

profile of v1, /device:TPU:1, one launch (start us, length us, event | category | flops | bytes accessed | tf_op | source)
XLA Modules:
  0.0 636.7 jit_solution(3507368074697231272)
XLA Ops:
  14.1 3.8 collective-permute-start
  17.9 11.9 %collective-permute-done = bf16[1,2,384,352]{2,3,1,0:T(8,128)(2,1)} collective-permute-done((bf16[1,2,384,352]{2,3,1,0:T(8,128)(2,1)S(1)}, bf16[1,2,384,352]{2,3,1,0:T(8,128)(2,1)}, u32[]{:S(2)}, u32[]{:S(2)}) %collective-permute-start) | collective-permute-done | bytes 540704 | tf_op jit(solution)/shard_map/ppermute | solution.py:28
  33.3 23.1 %collective-permute-done.1 = bf16[2,2,384,352]{2,3,1,0:T(8,128)(2,1)} collective-permute-done((bf16[2,2,384,352]{2,3,1,0:T(8,128)(2,1)}, bf16[2,2,384,352]{2,3,1,0:T(8,128)(2,1)}, u32[]{:S(2)}, u32[]{:S(2)}) %collective-permute-start.1) | collective-permute-done | bytes 1081376 | tf_op jit(solution)/shard_map/ppermute | solution.py:28
  56.4 4.0 maximum_select_fusion.1
  68.0 40.4 %collective-permute-done.2 = bf16[4,2,384,352]{2,3,1,0:T(8,128)(2,1)} collective-permute-done((bf16[4,2,384,352]{2,3,1,0:T(8,128)(2,1)}, bf16[4,2,384,352]{2,3,1,0:T(8,128)(2,1)}, u32[]{:S(2)}, u32[]{:S(2)}) %collective-permute-start.2) | collective-permute-done | bytes 2162720 | tf_op jit(solution)/shard_map/ppermute | solution.py:28
  108.5 3.9 fusion.22
  116.3 4.2 reshape.477
  120.5 3.7 copy.35
  124.2 4.7 reshape.478
  128.9 11.2 %fusion.16 = (f32[4,384]{1,0:T(4,128)S(1)}, f32[4,384,3072]{2,1,0:T(8,128)}) fusion(pred[3072]{0:T(1024)(128)(4,1)S(1)} %lt.153, bf16[384,4,88]{0,2,1:T(8,128)(2,1)S(1)} %bitcast.135, bf16[3072,4,88]{0,2,1:T(8,128)(2,1)} %reshape.477), kind=kOutput, calls=%fused_computation.24 | convolution fusion | flops 844626432 | bytes 21316608 | tf_op jit(solution)/shard_map/cqhe,ckhe->chqk/dot_general | solution.py:48
  140.1 11.2 %fusion.17 = f32[4,384]{1,0:T(4,128)S(1)} fusion(f32[4,384,3072]{2,1,0:T(8,128)} %get-tuple-element.87, f32[4,384]{1,0:T(4,128)S(1)} %get-tuple-element.85, pred[3072]{0:T(1024)(128)(4,1)S(1)} %lt.153), kind=kLoop, calls=%fused_computation.25 | loop fusion | flops 23591424 | bytes 18889728 | tf_op jit(solution)/shard_map/reduce_sum | solution.py:54
  151.4 12.2 %fusion.62 = bf16[384,4,88]{0,2,1:T(8,128)(2,1)} fusion(bf16[3072,4,88]{0,2,1:T(8,128)(2,1)} %reshape.478, f32[4,384,3072]{2,1,0:T(8,128)} %get-tuple-element.87, f32[4,384]{1,0:T(4,128)S(1)} %get-tuple-element.85, pred[3072]{0:T(1024)(128)(4,1)S(1)} %lt.153, f32[384,4]{0,1:T(4,128)S(1)} %bitcast_add_fusion.1, f32[384,4]{0,1:T(4,128)S(1)} %get-tuple-element.84), kind=kOutput, calls=%fused_computation.86 | convolution fusion | flops 854470656 | bytes 21328896 | tf_op jit(solution)/shard_map/chqk,ckhe->chqe/dot_general | solution.py:56
  168.7 10.2 %all-to-all-start = ((s32[32,1,12]{2,1,0:T(1,128)}), s32[32,1,12]{2,1,0:T(1,128)S(1)}, u32[]{:S(2)}, u32[]{:S(2)}) async-start(s32[32,1,12]{2,1,0:T(1,128)} %bitcast.3), calls=%async_computation | async-start | bytes 32768 | tf_op jit(solution)/shard_map/all_to_all | solution.py:172
  179.9 36.2 %all-reduce.2.cloned.1.call-done = bf16[384,1408]{1,0:T(8,128)(2,1)} async-done(((bf16[384,1408]{1,0:T(8,128)(2,1)}), bf16[384,1408]{1,0:T(8,128)(2,1)}) %all-reduce.2.cloned.1.call-update) | async-done | bytes 1081360 | tf_op jit(solution)/shard_map/psum | solution.py:133
  221.6 9.3 %all-to-all-start.1 = ((bf16[32,12,512]{2,1,0:T(8,128)(2,1)}), bf16[32,12,512]{2,1,0:T(8,128)(2,1)S(1)}, u32[]{:S(2)}, u32[]{:S(2)}) async-start(bf16[32,12,512]{2,1,0:T(8,128)(2,1)} %reshape.479), calls=%async_computation.1 | async-start | bytes 1048576 | tf_op jit(solution)/shard_map/all_to_all | solution.py:171
  231.0 3.7 fusion.57
  236.2 6.3 all-to-all-done.1
  242.6 4.0 scatter_custom_fusion
  246.6 3.0 fusion.23
  257.6 108.6 %all-gather.3.cloned.1.call-done = bf16[64,4,512,128]{3,2,1,0:T(8,128)(2,1)} async-done(((bf16[2,4,512,128]{3,2,1,0:T(8,128)(2,1)}), bf16[64,4,512,128]{3,2,1,0:T(8,128)(2,1)}) %all-gather.3.cloned.1.call-update) | async-done | bytes 33554448 | tf_op jit(solution)/shard_map/all_gather | solution.py:215
  366.1 44.2 %copy.36 = bf16[2,4,32,512,128]{3,4,1,0,2:T(8,128)(2,1)} copy(bf16[2,4,32,512,128]{4,3,1,0,2:T(8,128)(2,1)} %bitcast.130) | data formatting | bytes 67108864 | tf_op jit(solution)/shard_map/reshape | solution.py:215
  410.3 217.1 %while.15 = (s32[]{:T(128)}, f32[4,2,512]{2,1,0:T(2,128)S(1)}, f32[4,2,512]{2,1,0:T(2,128)S(1)}, f32[4,2,512,64]{2,3,1,0:T(8,128)S(1)}, bf16[32,2,4,512,2,64]{3,...) while((s32[]{:T(128)}, f32[4,2,512]{2,1,0:T(2,128)S(1)}, ...), condition=%wide.region_19.20_spmd.clone, body=%wide.region_16.19_spmd.clone.sunk | while | flops 554455040 | bytes 29098120 | solution.py:230
  427.7 2.9 fusion.145
  448.1 2.9 fusion.145
  454.9 2.9 fusion.145
  475.2 2.9 fusion.145
  495.6 2.9 fusion.145
  522.7 2.9 fusion.145
  543.1 2.9 fusion.145
  570.2 2.9 fusion.145
  590.6 2.9 fusion.145
  617.7 2.9 fusion.145
  (280 shorter events, 232.3 us)
Async XLA Ops:
  6.5 211.8 %copy-start = (bf16[1408,512]{1,0:T(8,128)(2,1)S(1)}, bf16[1408,512]{1,0:T(8,128)(2,1)}, u32[]{:S(2)}) copy-start(bf16[1408,512]{1,0:T(8,128)(2,1)} %param.25) | copy-start | bytes 4325380
  6.5 3.3 copy-start.4
  6.5 3.3 copy-start.12
  6.5 3.3 copy-start.13
  6.5 209.5 %all-reduce.2.cloned.1.call-start = ((), (), s32[]{:S(2)}) async-start(), calls=%async_computation.2 | async-start | bytes 2162688 | tf_op jit(solution)/shard_map/psum | solution.py:133
  14.1 15.7 %collective-permute-start = (bf16[1,2,384,352]{2,3,1,0:T(8,128)(2,1)S(1)}, bf16[1,2,384,352]{2,3,1,0:T(8,128)(2,1)}, u32[]{:S(2)}, u32[]{:S(2)}) collective-permute-start(bf16[1,2,384,352]{2,3,1,0:T(8,128)(2,1)S(1)} %maximum_bitcast_fusion), channel_id=1, source_target_pairs={{0,16},{16,0},{4,20},{20,4},{8,24},{24,8},{12,28},{28,12},{32,48},... | collective-permute-start | bytes 1622024 | tf_op jit(solution)/shard_map/ppermute | solution.py:28
  32.2 24.3 %collective-permute-start.1 = (bf16[2,2,384,352]{2,3,1,0:T(8,128)(2,1)}, bf16[2,2,384,352]{2,3,1,0:T(8,128)(2,1)}, u32[]{:S(2)}, u32[]{:S(2)}) collective-permute-start(bf16[2,2,384,352]{2,3,1,0:T(8,128)(2,1)} %maximum_select_fusion.2), channel_id=1, source_target_pairs={{0,32},{32,0},{4,36},{36,4},{8,40},{40,8},{12,44},{44,12},{16,48},... | collective-permute-start | bytes 3244040 | tf_op jit(solution)/shard_map/ppermute | solution.py:28
  33.3 31.1 %copy-start.11 = (s32[4,96]{1,0:T(4,128)S(1)}, s32[4,96]{1,0:T(4,128)}, u32[]{:S(2)}) copy-start(s32[4,96]{1,0:T(4,128)} %param.18) | copy-start | bytes 4612
  60.4 48.1 %collective-permute-start.2 = (bf16[4,2,384,352]{2,3,1,0:T(8,128)(2,1)}, bf16[4,2,384,352]{2,3,1,0:T(8,128)(2,1)}, u32[]{:S(2)}, u32[]{:S(2)}) collective-permute-start(bf16[4,2,384,352]{2,3,1,0:T(8,128)(2,1)} %maximum_select_fusion.1), channel_id=1, source_target_pairs={{0,64},{64,0},{4,68},{68,4},{8,72},{72,8},{12,76},{76,12},{16,80},... | collective-permute-start | bytes 6488072 | tf_op jit(solution)/shard_map/ppermute | solution.py:28
  151.4 12.2 %copy-start.6 = (bf16[352,1408]{1,0:T(8,128)(2,1)S(1)}, bf16[352,1408]{1,0:T(8,128)(2,1)}, u32[]{:S(2)}) copy-start(bf16[352,1408]{1,0:T(8,128)(2,1)} %param.22) | copy-start | bytes 2973700
  168.7 52.9 %all-to-all-start = ((s32[32,1,12]{2,1,0:T(1,128)}), s32[32,1,12]{2,1,0:T(1,128)S(1)}, u32[]{:S(2)}, u32[]{:S(2)}) async-start(s32[32,1,12]{2,1,0:T(1,128)} %bitcast.3), calls=%async_computation | async-start | bytes 32768 | tf_op jit(solution)/shard_map/all_to_all | solution.py:172
  179.8 38.5 %copy-start.14 = (f32[1408]{0:T(1024)S(1)}, f32[1408]{0:T(1024)}, u32[]{:S(2)}) copy-start(f32[1408]{0:T(1024)} %param.24) | copy-start | bytes 16900
  179.8 38.5 %copy-start.15 = (f32[1408]{0:T(1024)S(1)}, f32[1408]{0:T(1024)}, u32[]{:S(2)}) copy-start(f32[1408]{0:T(1024)} %param.23) | copy-start | bytes 16900
  216.1 1.7 copy-start.5
  221.6 20.9 %all-to-all-start.1 = ((bf16[32,12,512]{2,1,0:T(8,128)(2,1)}), bf16[32,12,512]{2,1,0:T(8,128)(2,1)S(1)}, u32[]{:S(2)}, u32[]{:S(2)}) async-start(bf16[32,12,512]{2,1,0:T(8,128)(2,1)} %reshape.479), calls=%async_computation.1 | async-start | bytes 1048576 | tf_op jit(solution)/shard_map/all_to_all | solution.py:171
  230.9 135.2 %all-gather.3.cloned.1.call-start = ((), (), s32[]{:S(2)}) async-start(), calls=%async_computation.3 | async-start | bytes 34603008 | tf_op jit(solution)/shard_map/all_gather | solution.py:215
  242.6 4.0 copy-start.8
  246.6 3.4 copy-start.2
  250.0 1.3 copy-start.9
  250.0 1.3 copy-start.10
  251.4 1.2 copy-start.7
  252.6 1.4 copy-start.3
  627.4 2.2 copy-start.1
Sparse Core Ops, SparseCore 0:
  166.5 49.5 all-reduce.1
  255.2 110.8 all-gather.2
